TPU v7x, 128 devices: a whole 4x4x4 slice. The times are simulated.
128 devices in a mesh: head: 8 (over z, core), query: 8 (over x, y_lo), ctx: 2 (over y_hi).
Axes of the slice: x: 4, y: 4 (y_hi: 2, y_lo: 2; y = y_hi * 2 + y_lo), z: 4, core: 2. Of those that a mesh axis runs over, the one named last changes fastest.
Arguments:
- queries: bfloat16 [1024, 128, 576], P('query', 'head'), may hold values from -3 to 3, as said below
- latent: bfloat16 [4096, 576], P(('head', 'query', 'ctx')), may hold values from -8 to 8
- out_grad: bfloat16 [1024, 128, 512], P('query', 'head'), may hold values from -6 to 6
- log_norms: float32 [1024, 128], P('query', 'head'), as said below
- row_dots: float32 [1024, 128], P('query', 'head'), may hold values from -48 to 48
Outputs:
- query_grad: float32 [1024, 128, 576], P(('query', 'ctx'), 'head')
- latent_grad: float32 [4096, 576], P(('head', 'query', 'ctx'))
Inputs may be any that keep to these rules, and one draw needn't show every extreme that they name: queries and latent are of order one; latent rows may differ in scale. log_norms[i,h] is the log of the sum over all 4096 latent rows of exp(scores[i,h,j]), computed from the given queries and latent.
All inputs are finite; a program needn't handle non-finite values.
Results may differ from a plain program's by a relative error of at most 0.0029.
Values may be sent and summed in bfloat16 or wider, within the bound.
No kernel may reach another device: no remote copies, remote signals or barrier semaphores. Data moves between devices by JAX's collectives and lax.ppermute only.
A program may use at most 64 MiB of HBM per device.

v0:
```python
import math
import jax
import jax.numpy as jnp
from jax import lax
from jax.sharding import PartitionSpec as P

softmax_scale = 192.0 ** (-0.5) * (0.1 * math.log(40.0) + 1.0) ** 2


def tile_grads(flat_q, flat_dout, norms, dots, latent_block):
    value_width = flat_dout.shape[1]
    key_width = latent_block.shape[1]
    scores = (
        lax.dot_general(
            flat_q, latent_block, (((1,), (1,)), ((), ())), preferred_element_type=jnp.float32
        )
        * softmax_scale
    )
    probs = jnp.exp(scores - norms[:, None])
    probs_low = probs.astype(jnp.bfloat16)
    dprobs = lax.dot_general(
        flat_dout,
        latent_block[:, :value_width],
        (((1,), (1,)), ((), ())),
        preferred_element_type=jnp.float32,
    )
    dscores = (probs * (dprobs - dots[:, None])).astype(jnp.bfloat16)
    query_part = jnp.dot(dscores, latent_block, preferred_element_type=jnp.float32)
    latent_key = (
        lax.dot_general(
            dscores, flat_q, (((0,), (0,)), ((), ())), preferred_element_type=jnp.float32
        )
        * softmax_scale
    )
    latent_value = lax.dot_general(
        probs_low, flat_dout, (((0,), (0,)), ((), ())), preferred_element_type=jnp.float32
    )
    latent_part = latent_key + jnp.pad(latent_value, ((0, 0), (0, key_width - value_width)))
    return (query_part, latent_part)


def span_grads(flat_q, flat_dout, norms, dots, latent_rows):
    row_count = latent_rows.shape[0]
    key_width = latent_rows.shape[1]
    block_rows = 512
    stacked = latent_rows.reshape(row_count // block_rows, block_rows, key_width)

    def single(carry, latent_block):
        query_part, latent_part = tile_grads(flat_q, flat_dout, norms, dots, latent_block)
        return (carry + query_part, latent_part)

    initial = jnp.zeros((flat_q.shape[0], key_width), jnp.float32)
    query_sum, latent_parts = lax.scan(single, initial, stacked)
    return (query_sum, latent_parts.reshape(row_count, key_width))


def on_device(queries, latent, out_grad, log_norms, row_dots):
    local_queries, local_heads, key_width = queries.shape
    flat_rows = local_queries * local_heads
    flat_q = queries.reshape(flat_rows, key_width)
    flat_dout = out_grad.reshape(flat_rows, out_grad.shape[2])
    norms = log_norms.reshape(flat_rows)
    dots = row_dots.reshape(flat_rows)
    gathered = lax.all_gather(latent, ("head", "query"), axis=0, tiled=True)
    query_sum, latent_all = span_grads(flat_q, flat_dout, norms, dots, gathered)
    latent_grad = lax.psum_scatter(latent_all, ("head", "query"), scatter_dimension=0, tiled=True)
    query_terms = (query_sum * softmax_scale).reshape(local_queries, local_heads, key_width)
    query_grad = lax.psum_scatter(query_terms, "ctx", scatter_dimension=0, tiled=True)
    return (query_grad, latent_grad)


def solution(mesh):
    in_specs = (
        P("query", "head", None),
        P(("head", "query", "ctx"), None),
        P("query", "head", None),
        P("query", "head"),
        P("query", "head"),
    )
    out_specs = (P(("query", "ctx"), "head", None), P(("head", "query", "ctx"), None))
    return jax.shard_map(
        on_device, mesh=mesh, in_specs=in_specs, out_specs=out_specs, check_vma=False
    )
```

profile of v0, /device:TPU:1, one launch (start us, length us, event | category | flops | bytes accessed | tf_op | source)
XLA Modules:
  0.0 596.4 jit_solution(4269715359291730156)
XLA Ops:
  9.7 3.9 copy.10
  13.7 157.6 %all-gather.2.cloned.1.call-done = bf16[2048,576]{1,0:T(8,128)(2,1)} async-done(((bf16[32,576]{1,0:T(8,128)(2,1)}), bf16[2048,576]{1,0:T(8,128)(2,1)}) %all-gather.2.cloned.1.call-update) | async-done | bytes 2359312 | tf_op jit(solution)/shard_map/all_gather | solution.py:64
  171.3 49.7 %while.16 = (s32[]{:T(128)}, f32[2048,576]{0,1:T(8,128)}, f32[4,512,576]{1,2,0:T(8,128)}, bf16[4,512,576]{2,1,0:T(8,128)(2,1)}, bf16[2048,576]{1,0:T(8,128)(2,1)...) while((s32[]{:T(128)}, f32[2048,576]{0,1:T(8,128)}, ...), condition=%wide.wide.region_1.2_spmd.clone, body=%wide.wide.region_0.1_spmd.clone.sunk | while | flops 5782700032 | bytes 84828408 | solution.py:53
  172.4 1.8 fusion.55
  174.3 1.3 fusion.56
  175.6 1.3 multiply_convert_fusion.3
  177.0 2.4 fusion.57
  179.4 2.1 select_add_fusion.3
  181.6 2.1 copy-done
  184.9 1.8 fusion.55
  186.7 1.3 fusion.56
  188.0 1.3 multiply_convert_fusion.3
  189.4 2.4 fusion.57
  191.8 2.1 select_add_fusion.3
  194.0 2.1 copy-done
  197.3 1.8 fusion.55
  199.1 1.3 fusion.56
  200.4 1.3 multiply_convert_fusion.3
  201.8 2.5 fusion.57
  204.3 2.1 select_add_fusion.3
  206.4 2.1 copy-done
  209.7 1.8 fusion.55
  211.6 1.3 fusion.56
  212.9 1.3 multiply_convert_fusion.3
  214.3 2.4 fusion.57
  216.7 2.1 select_add_fusion.3
  218.8 2.1 copy-done
  221.0 5.8 copy.14
  226.8 5.4 broadcast_multiply_fusion
  232.3 5.8 copy.13
  238.1 272.0 %reduce-scatter.5.cloned.1.call-done = f32[32,576]{1,0:T(8,128)} async-done(((f32[2048,576]{1,0:T(8,128)}), f32[32,576]{1,0:T(8,128)}) %reduce-scatter.5.cloned.1.call-update) | async-done | bytes 73744 | tf_op jit(solution)/shard_map/reduce_scatter | solution.py:66
  510.1 79.8 %reduce-scatter.3.cloned.1.call-done = f32[64,16,576]{2,1,0:T(8,128)} async-done(((f32[128,16,576]{2,1,0:T(8,128)}), f32[64,16,576]{2,1,0:T(8,128)}) %reduce-scatter.3.cloned.1.call-update) | async-done | bytes 2359312 | tf_op jit(solution)/shard_map/reduce_scatter | solution.py:68
  (52 shorter events, 7.3 us)
Async XLA Ops:
  7.2 164.1 %all-gather.2.cloned.1.call-start = ((), (), s32[]{:S(2)}) async-start(), calls=%async_computation.2 | async-start | bytes 2662400 | tf_op jit(solution)/shard_map/all_gather | solution.py:64
  7.9 502.2 %reduce-scatter.5.cloned.1.call-start = ((), (), s32[]{:S(2)}) async-start(), calls=%async_computation.4 | async-start | bytes 5324800 | tf_op jit(solution)/shard_map/reduce_scatter | solution.py:66
  8.8 162.5 %copy-start.1 = (f32[128,16]{1,0:T(8,128)}, f32[128,16]{1,0:T(8,128)S(1)}, u32[]{:S(2)}) copy-start(f32[128,16]{1,0:T(8,128)S(1)} %copy.11) | copy-start | bytes 24580
  9.6 161.6 %copy-start.2 = (f32[128,16]{1,0:T(8,128)}, f32[128,16]{1,0:T(8,128)S(1)}, u32[]{:S(2)}) copy-start(f32[128,16]{1,0:T(8,128)S(1)} %copy.12) | copy-start | bytes 24580
  172.4 1.8 copy-start.3
  175.6 3.8 slice-start
  177.0 2.5 slice-start.1
  181.6 2.1 copy-start
  184.8 1.8 copy-start.3
  188.0 3.8 slice-start
  189.4 2.5 slice-start.1
  194.0 2.1 copy-start
  197.3 1.8 copy-start.3
  200.4 3.9 slice-start
  201.8 2.5 slice-start.1
  206.4 2.1 copy-start
  209.7 1.8 copy-start.3
  212.9 3.8 slice-start
  214.3 2.5 slice-start.1
  218.8 2.1 copy-start
  226.8 363.1 %reduce-scatter.3.cloned.1.call-start = ((), (), s32[]{:S(2)}) async-start(), calls=%async_computation.3 | async-start | bytes 7864320 | tf_op jit(solution)/shard_map/reduce_scatter | solution.py:68
Sparse Core Ops, SparseCore 0:
  9.7 161.5 all-gather.1
  226.9 283.1 reduce-scatter.4
  513.1 76.7 reduce-scatter.2
where the time goes:
time: 597 us; the launch traced here: 596 us
  waiting for transfers between devices  510 us (85%)
  matrix products  36.2 us (6%)
  local copies, waits for them, and re-layouts  30.5 us (5%)
  between operations  13.8 us (2%)
    reduce_scatter x1, waiting for transfers between devices, on_device(): lax.psum_scatter(latent_all, ('head', 'query'), scatter_dimension=0, tile...  272 us
    all_gather x1, waiting for transfers between devices, on_device(): gathered = lax.all_gather(latent, ('head', 'query'), axis=0, tiled=True)  158 us
    reduce_scatter x1, waiting for transfers between devices, on_device(): lax.psum_scatter(query_terms, 'ctx', scatter_dimension=0, tiled=True)  79.8 us
  transfers between devices with their start and end apart: 3, of which 3 were waited for; matrix products, arithmetic and copies ran while one was open for 3% of the time, Pallas kernels for 0%

commit v1 on v0

--- a/solution.py
+++ b/solution.py
@@ -1,3 +1,4 @@
+import functools
 import math
 import jax
 import jax.numpy as jnp
@@ -5,6 +6,16 @@
 from jax.sharding import PartitionSpec as P
 
 softmax_scale = 192.0 ** (-0.5) * (0.1 * math.log(40.0) + 1.0) ** 2
+
+
+def rows_define(vector, axis_id, dimension_no):
+    low = jax.lax.axis_size(axis_id)
+    e_next = jnp.stack([vector] * low, 0)
+    top = jax.lax.all_to_all(e_next, axis_id, 0, 0)
+    return jnp.concatenate(top, dimension_no)
+
+
+balance_the_racks = functools.partial(rows_define, axis_id=("head", "query"), dimension_no=0)
 
 
 def tile_grads(flat_q, flat_dout, norms, dots, latent_block):
@@ -61,7 +72,7 @@
     flat_dout = out_grad.reshape(flat_rows, out_grad.shape[2])
     norms = log_norms.reshape(flat_rows)
     dots = row_dots.reshape(flat_rows)
-    gathered = lax.all_gather(latent, ("head", "query"), axis=0, tiled=True)
+    gathered = balance_the_racks(latent)
     query_sum, latent_all = span_grads(flat_q, flat_dout, norms, dots, gathered)
     latent_grad = lax.psum_scatter(latent_all, ("head", "query"), scatter_dimension=0, tiled=True)
     query_terms = (query_sum * softmax_scale).reshape(local_queries, local_heads, key_width)

time: 597 us -> 485 us (0.81)
  waiting for transfers between devices: 510 us -> 380 us
  starting transfers between devices: 0.12 us -> 10.9 us
  matrix products: 36.2 us -> 43.8 us
    all_gather x1 -> x0, waiting for transfers between devices: 158 us -> none  [on_device(): gathered = lax.all_gather(latent, ('head', 'query'), axis=0, tiled=True)]
    all_to_all x0 -> x1, waiting for transfers between devices: none -> 29.2 us  [rows_define(): top = jax.lax.all_to_all(e_next, axis_id, 0, 0)]
    all_to_all x0 -> x1, starting transfers between devices: none -> 10.8 us  [rows_define(): top = jax.lax.all_to_all(e_next, axis_id, 0, 0)]
    dot_general x4, matrix products: 7.3 us -> 14.9 us  [tile_grads(): lax.dot_general(flat_q, latent_block, (((1,), (1,)), ((), ())), preferred...]
where the time goes in v1:
time: 485 us; the launch traced here: 484 us
  waiting for transfers between devices  380 us (78%)
  matrix products  43.8 us (9%)
  local copies, waits for them, and re-layouts  29.8 us (6%)
  between operations  14.1 us (3%)
  starting transfers between devices  10.9 us (2%)
  other arithmetic  5.44 us (1%)
    reduce_scatter x1, waiting for transfers between devices, on_device(): lax.psum_scatter(latent_all, ('head', 'query'), scatter_dimension=0, tile...  271 us
    reduce_scatter x1, waiting for transfers between devices, on_device(): lax.psum_scatter(query_terms, 'ctx', scatter_dimension=0, tiled=True)  79.1 us
    all_to_all x1, waiting for transfers between devices, rows_define(): top = jax.lax.all_to_all(e_next, axis_id, 0, 0)  29.2 us
    dot_general x4, matrix products, tile_grads(): lax.dot_general(flat_q, latent_block, (((1,), (1,)), ((), ())), preferred...  14.9 us
    all_to_all x1, starting transfers between devices, rows_define(): top = jax.lax.all_to_all(e_next, axis_id, 0, 0)  10.8 us
    while x40, local copies, waits for them, and re-layouts  10.2 us
    dot_general x4, matrix products, tile_grads(): lax.dot_general(dscores, flat_q, (((0,), (0,)), ((), ())), preferred_elem...  9.85 us
  transfers between devices with their start and end apart: 3, of which 3 were waited for; matrix products, arithmetic and copies ran while one was open for 3% of the time, Pallas kernels for 0%

profile of v1, /device:TPU:1, one launch (start us, length us, event | category | flops | bytes accessed | tf_op | source)
XLA Modules:
  0.0 484.0 jit_solution(8382426142184636010)
XLA Ops:
  7.2 2.5 stack.2
  9.7 10.8 %all-to-all-start = ((bf16[64,32,576]{2,1,0:T(8,128)(2,1)}), bf16[64,32,576]{2,1,0:T(8,128)(2,1)S(1)}, u32[]{:S(2)}, u32[]{:S(2)}) async-start(bf16[64,32,576]{2,1,0:T(8,128)(2,1)} %stack.2), calls=%async_computation | async-start | bytes 5242880 | tf_op jit(solution)/shard_map/all_to_all | solution.py:14
  21.0 4.9 %copy.10 = bf16[128,16,576]{2,1,0:T(8,128)(2,1)} copy(bf16[128,16,576]{0,2,1:T(8,128)(2,1)} %param.7) | data formatting | bytes 4718592 | tf_op args[0]
  25.9 29.2 %all-to-all-done = bf16[64,32,576]{2,1,0:T(8,128)(2,1)S(1)} async-done(((bf16[64,32,576]{2,1,0:T(8,128)(2,1)}), bf16[64,32,576]{2,1,0:T(8,128)(2,1)S(1)}, u32[]{:S(2)}, u32[]{:S(2)}) %all-to-all-start) | async-done | bytes 2359328 | tf_op jit(solution)/shard_map/all_to_all | solution.py:14
  55.1 54.6 %while.16 = (s32[]{:T(128)}, f32[2048,576]{0,1:T(8,128)}, f32[4,512,576]{1,2,0:T(8,128)}, bf16[4,512,576]{2,1,0:T(8,128)(2,1)S(1)}, bf16[2048,576]{1,0:T(8,128)(...) while((s32[]{:T(128)}, f32[2048,576]{0,1:T(8,128)}, ...), condition=%wide.wide.region_1.2_spmd.clone, body=%wide.wide.region_0.1_spmd.clone.sunk | while | flops 5782700032 | bytes 94265624 | solution.py:64
  55.2 3.7 fusion.55
  60.3 1.3 multiply_convert_fusion.3
  62.0 2.4 fusion.57
  64.5 2.1 select_add_fusion.3
  66.6 2.2 copy-done
  68.8 3.7 fusion.55
  72.6 1.3 fusion.56
  73.9 1.3 multiply_convert_fusion.3
  75.6 2.4 fusion.57
  78.1 2.1 select_add_fusion.3
  80.2 2.2 copy-done
  82.5 3.7 fusion.55
  86.2 1.3 fusion.56
  87.5 1.3 multiply_convert_fusion.3
  89.3 2.5 fusion.57
  91.8 2.1 select_add_fusion.3
  93.9 2.2 copy-done
  96.2 3.7 fusion.55
  101.2 1.3 multiply_convert_fusion.3
  103.0 2.4 fusion.57
  105.4 2.1 select_add_fusion.3
  107.5 2.2 copy-done
  109.7 5.8 %copy.14 = f32[4,512,576]{2,1,0:T(8,128)} copy(f32[4,512,576]{1,2,0:T(8,128)} %get-tuple-element.105) | data formatting | bytes 9437184 | tf_op jit(solution)/shard_map/while | solution.py:64
  115.5 5.4 %broadcast_multiply_fusion = f32[2048,576]{0,1:T(8,128)} fusion(f32[2048,576]{0,1:T(8,128)} %get-tuple-element.104), kind=kLoop, calls=%fused_computation.14 | loop fusion | flops 1179648 | bytes 9437184 | tf_op jit(solution)/shard_map/mul | solution.py:78
  121.0 5.8 %copy.13 = f32[2048,576]{1,0:T(8,128)} copy(f32[2048,576]{0,1:T(8,128)} %broadcast_multiply_fusion) | data formatting | bytes 9437184 | tf_op jit(solution)/shard_map/mul | solution.py:78
  126.8 271.3 %reduce-scatter.5.cloned.1.call-done = f32[32,576]{1,0:T(8,128)} async-done(((f32[2048,576]{1,0:T(8,128)}), f32[32,576]{1,0:T(8,128)}) %reduce-scatter.5.cloned.1.call-update) | async-done | bytes 73744 | tf_op jit(solution)/shard_map/reduce_scatter | solution.py:77
  398.1 79.1 %reduce-scatter.3.cloned.1.call-done = f32[64,16,576]{2,1,0:T(8,128)} async-done(((f32[128,16,576]{2,1,0:T(8,128)}), f32[64,16,576]{2,1,0:T(8,128)}) %reduce-scatter.3.cloned.1.call-update) | async-done | bytes 2359312 | tf_op jit(solution)/shard_map/reduce_scatter | solution.py:79
  (64 shorter events, 4.9 us)
Async XLA Ops:
  7.2 13.4 %copy-start.4 = (f32[128,16]{0,1:T(8,128)S(1)}, f32[128,16]{0,1:T(8,128)}, u32[]{:S(2)}) copy-start(f32[128,16]{0,1:T(8,128)} %param.10) | copy-start | bytes 24580
  7.2 13.6 %copy-start.5 = (f32[128,16]{0,1:T(8,128)S(1)}, f32[128,16]{0,1:T(8,128)}, u32[]{:S(2)}) copy-start(f32[128,16]{0,1:T(8,128)} %param.11) | copy-start | bytes 24580
  9.7 45.5 %all-to-all-start = ((bf16[64,32,576]{2,1,0:T(8,128)(2,1)}), bf16[64,32,576]{2,1,0:T(8,128)(2,1)S(1)}, u32[]{:S(2)}, u32[]{:S(2)}) async-start(bf16[64,32,576]{2,1,0:T(8,128)(2,1)} %stack.2), calls=%async_computation | async-start | bytes 5242880 | tf_op jit(solution)/shard_map/all_to_all | solution.py:14
  20.5 377.5 %reduce-scatter.5.cloned.1.call-start = ((), (), s32[]{:S(2)}) async-start(), calls=%async_computation.4 | async-start | bytes 5324800 | tf_op jit(solution)/shard_map/reduce_scatter | solution.py:77
  20.7 34.4 %copy-start.2 = (f32[128,16]{1,0:T(8,128)}, f32[128,16]{1,0:T(8,128)S(1)}, u32[]{:S(2)}) copy-start(f32[128,16]{1,0:T(8,128)S(1)} %copy.11) | copy-start | bytes 24580
  20.9 34.2 %copy-start.3 = (f32[128,16]{1,0:T(8,128)}, f32[128,16]{1,0:T(8,128)S(1)}, u32[]{:S(2)}) copy-start(f32[128,16]{1,0:T(8,128)S(1)} %copy.12) | copy-start | bytes 24580
  55.2 3.7 copy-start.6
  60.3 1.7 copy-start.1
  60.3 4.2 slice-start
  62.0 2.4 slice-start.1
  66.6 2.2 copy-start
  68.8 3.7 copy-start.6
  73.9 1.7 copy-start.1
  73.9 4.2 slice-start
  75.6 2.5 slice-start.1
  80.2 2.2 copy-start
  82.4 3.7 copy-start.6
  87.5 1.7 copy-start.1
  87.5 4.3 slice-start
  89.3 2.5 slice-start.1
  93.9 2.2 copy-start
  96.2 3.7 copy-start.6
  101.2 1.7 copy-start.1
  101.2 4.2 slice-start
  103.0 2.4 slice-start.1
  107.5 2.2 copy-start
  115.5 361.6 %reduce-scatter.3.cloned.1.call-start = ((), (), s32[]{:S(2)}) async-start(), calls=%async_computation.3 | async-start | bytes 7864320 | tf_op jit(solution)/shard_map/reduce_scatter | solution.py:79
Sparse Core Ops, SparseCore 0:
  115.6 282.4 reduce-scatter.4
  401.1 76.0 reduce-scatter.2
